TPU v7x, 768 devices: a whole 4x8x12 slice. The times are simulated.
768 devices in a mesh: dp: 192 (over z, y, core), tensor: 4 (over x).
Axes of the slice: x: 4, y: 8, z: 12, core: 2. Of those that a mesh axis runs over, the one named last changes fastest.
Arguments:
- hidden: bfloat16 [24576, 8192], P('dp'), may hold values from -50 to 50
- gain: float32 [8192], replicated, may hold values from 0.5 to 1.5
- w_key: bfloat16 [8192, 512], P(None, 'tensor'), may hold values from -3 to 3
- grad_key: bfloat16 [24576, 512], P('dp', 'tensor'), may hold values from -0.119628906 to 0.119628906
- counts: int32 [192], P('dp'), may hold values from 32 to 128, as said below
Outputs:
- key_grad: float32 [8256, 512], P('dp', 'tensor')
- normed_grad: bfloat16 [24576, 8192], P('dp', 'tensor')
Inputs may be any that keep to these rules, and one draw needn't show every extreme that they name: Tokens past counts of a bin are padding. At least one bin is full and one holds exactly 32 real tokens.
All inputs are finite; a program needn't handle non-finite values.
Results may differ from a plain program's by a relative error of at most 0.012.
Values may be sent and summed in bfloat16 or wider, within the bound.
A program may use at most 32 MiB of HBM per device.

v0:
```python
import functools

import jax
import jax.numpy as jnp
from jax import lax
from jax.sharding import Mesh
from jax.sharding import PartitionSpec as P

DP = ("dp_0", "dp_1", "dp_2")


EPSILON = 1e-05


def one_axis_at_a_time(x, axes):
    return functools.reduce(lax.psum, axes, x)


def cut_along(x, dim, devices):
    before, after = (x.shape[:dim], x.shape[dim + 1 :])
    return jnp.moveaxis(x.reshape(*before, devices, -1, *after), dim, 0)


def own_tiles(x, axis, dim):
    devices = lax.axis_size(axis)
    tiles = cut_along(x, dim, devices)
    lines = tiles.reshape(devices, -1)
    span = max(16, -(-lines.shape[1] // 1024) * 8)
    lines = jnp.pad(lines, ((0, 0), (0, span * 128 - lines.shape[1]))).reshape(-1, 128)
    own = lax.psum_scatter(lines, axis, scatter_dimension=0, tiled=True)
    return own.reshape(-1)[: tiles[0].size].reshape(tiles.shape[1:])


def sent_and_summed(x, axis, dim):
    devices = lax.axis_size(axis)
    tiles = lax.all_to_all(cut_along(x, dim, devices), axis, 0, 0, tiled=True)
    return jnp.sum(tiles.astype(jnp.float32), axis=0)


def per_device(hidden, gain, w_key, grad_key, counts):
    tok_rows = hidden.shape[0]
    feature_width = hidden.shape[1]
    data_shards = lax.axis_size(DP)
    block_rows = -(-feature_width // data_shards)
    pad_rows = block_rows * data_shards - feature_width
    wide_hidden = hidden.astype(jnp.float32)
    inv_rms = lax.rsqrt(jnp.mean(wide_hidden * wide_hidden, axis=1, keepdims=True) + EPSILON)
    normed = (wide_hidden * inv_rms * gain).astype(jnp.bfloat16)
    live_rows = jnp.arange(tok_rows) < counts[0]
    masked_key = jnp.where(live_rows[:, None], grad_key, jnp.zeros((), jnp.bfloat16))
    padded = jnp.pad(normed, ((0, 0), (0, pad_rows)))
    contract = (((0,), (0,)), ((), ()))
    own_count = jnp.sum(counts.astype(jnp.float32))
    real_total = one_axis_at_a_time(own_count, DP)
    summed_key = own_tiles(
        lax.dot_general(padded, masked_key, contract, preferred_element_type=jnp.float32), DP, 0
    )
    weighting = jnp.float32(tok_rows * data_shards) / real_total
    key_grad = summed_key * weighting
    partial_value = lax.dot_general(
        masked_key, w_key, (((1,), (1,)), ((), ())), preferred_element_type=jnp.float32
    ).astype(jnp.bfloat16)
    summed = sent_and_summed(partial_value, "tensor", 1)
    normed_grad = (summed * weighting).astype(jnp.bfloat16)
    return (key_grad, normed_grad)


def solution(mesh):
    split = Mesh(
        mesh.devices.reshape(12, 8, 2, mesh.shape["tensor"]), ("dp_0", "dp_1", "dp_2", "tensor")
    )
    return jax.shard_map(
        per_device,
        mesh=split,
        in_specs=(P(DP, None), P(), P(None, "tensor"), P(DP, "tensor"), P(DP)),
        out_specs=(P(DP, "tensor"), P(DP, "tensor")),
        check_vma=False,
    )
```

profile of v0, /device:TPU:1, one launch (start us, length us, event | category | flops | bytes accessed | tf_op | source)
XLA Modules:
  0.0 353.6 jit_solution(8397260693840256560)
XLA Ops:
  7.2 0.0 copy-start
  7.2 0.0 reduce-scatter.2.cloned.1.call-start
  7.2 0.0 copy-start.1
  8.0 2.2 fusion
  10.2 0.0 copy-start.2
  10.3 0.0 copy-done.1
  10.3 1.3 fusion.2
  11.6 0.0 copy-done.2
  11.6 2.8 fusion.3
  14.4 5.0 %reshape_reshape.3 = f32[192,5504]{1,0:T(8,128)} reshape(f32[8256,128]{1,0:T(8,128)} %fusion.3) | data formatting | bytes 8454144 | tf_op jit(solution)/shard_map/reshape;reshape | solution.py:27
  19.4 4.9 %pad.9 = f32[192,6144]{1,0:T(8,128)} pad(f32[192,5504]{1,0:T(8,128)} %reshape_reshape.3, f32[]{:T(128)} %constant.5.clone.1), padding=0_0x0_640 | pad | bytes 8945668 | tf_op jit(solution)/shard_map/jit(_pad)/pad | solution.py:29
  24.3 5.2 %reshape.28 = f32[9216,128]{1,0:T(8,128)} reshape(f32[192,6144]{1,0:T(8,128)} %pad.9) | data formatting | bytes 9437184 | tf_op jit(solution)/shard_map/reshape | solution.py:29
  29.5 0.0 reduce-scatter.2.cloned.1.call-update
  29.5 0.0 copy-done
  29.5 0.7 convolution_convert_fusion
  30.3 1.5 copy.10
  31.8 4.8 %all-to-all-start = ((bf16[4,128,2048]{2,1,0:T(8,128)(2,1)}), bf16[4,128,2048]{2,1,0:T(8,128)(2,1)}, u32[]{:S(2)}, u32[]{:S(2)}) async-start(bf16[4,128,2048]{2,1,0:T(8,128)(2,1)} %bitcast.11), calls=%async_computation.1 | async-start | bytes 4194304 | tf_op jit(solution)/shard_map/all_to_all | solution.py:36
  36.6 31.4 %psum.21 = f32[]{:T(128)} all-reduce(f32[]{:T(128)} %bitcast.1), channel_id=1, replica_groups=mesh['dp_0'=12,'dp_1'=8,'dp_2'=2,'tensor'=4] {'dp_0'}, use_global_device_ids=true, to_apply=%region_2.3 | all-reduce | flops 1 | bytes 8 | tf_op jit(solution)/shard_map/psum | solution.py:16
  68.0 14.8 %psum.22 = f32[]{:T(128)} all-reduce(f32[]{:T(128)} %psum.21), channel_id=1, replica_groups=mesh['dp_0'=12,'dp_1'=8,'dp_2'=2,'tensor'=4] {'dp_1'}, use_global_device_ids=true, to_apply=%region_3.4 | all-reduce | flops 1 | bytes 8 | tf_op jit(solution)/shard_map/psum | solution.py:16
  82.8 10.4 %psum.23 = f32[]{:T(128)} all-reduce(f32[]{:T(128)} %psum.22), channel_id=1, replica_groups=mesh['dp_0'=12,'dp_1'=8,'dp_2'=2,'tensor'=4] {'dp_2'}, use_global_device_ids=true, to_apply=%region_4.5 | all-reduce | flops 1 | bytes 8 | tf_op jit(solution)/shard_map/psum | solution.py:16
  93.8 0.0 all-to-all-done
  93.9 2.1 convert_reduce_fusion
  96.0 0.9 multiply_convert_fusion
  96.9 248.5 %reduce-scatter.2.cloned.1.call-done = f32[48,128]{1,0:T(8,128)} async-done(((f32[9216,128]{1,0:T(8,128)}), f32[48,128]{1,0:T(8,128)}) %reduce-scatter.2.cloned.1.call-update) | async-done | bytes 24592 | tf_op jit(solution)/shard_map/reduce_scatter | solution.py:30
  345.4 1.3 slice_multiply_fusion
  (2 shorter events, 0.0 us)
Async XLA Ops:
  7.2 22.4 %copy-start = (bf16[8192,128]{1,0:T(8,128)(2,1)S(1)}, bf16[8192,128]{1,0:T(8,128)(2,1)}, u32[]{:S(2)}) copy-start(bf16[8192,128]{1,0:T(8,128)(2,1)} %param.7) | copy-start | bytes 6291460
  7.2 338.2 %reduce-scatter.2.cloned.1.call-start = ((), (), s32[]{:S(2)}) async-start(), calls=%async_computation.2 | async-start | bytes 4743168 | tf_op jit(solution)/shard_map/reduce_scatter | solution.py:30
  7.2 3.0 copy-start.1
  10.2 1.4 copy-start.2
  31.8 62.0 %all-to-all-start = ((bf16[4,128,2048]{2,1,0:T(8,128)(2,1)}), bf16[4,128,2048]{2,1,0:T(8,128)(2,1)}, u32[]{:S(2)}, u32[]{:S(2)}) async-start(bf16[4,128,2048]{2,1,0:T(8,128)(2,1)} %bitcast.11), calls=%async_computation.1 | async-start | bytes 4194304 | tf_op jit(solution)/shard_map/all_to_all | solution.py:36
Sparse Core Ops, SparseCore 0:
  29.6 315.6 reduce-scatter.1
where the time goes:
time: 355 us; the launch traced here: 354 us
  waiting for transfers between devices  249 us (70%)
  blocking collectives  56.5 us (16%)
  local copies, waits for them, and re-layouts  16.7 us (5%)
  between operations  15.6 us (4%)
  other arithmetic  7.86 us (2%)
  starting transfers between devices  4.86 us (1%)
    reduce_scatter x1, waiting for transfers between devices, own_tiles(): own = lax.psum_scatter(lines, axis, scatter_dimension=0, tiled=True)  249 us
    psum x3, blocking collectives, one_axis_at_a_time(): return functools.reduce(lax.psum, axes, x)  56.5 us
  transfers between devices with their start and end apart: 2, of which 1 were waited for; matrix products, arithmetic and copies ran while one was open for 1% of the time, Pallas kernels for 0%

commit v1 on v0

v1 whole, which is shorter than its diff:
```python
import functools

import jax
import jax.numpy as jnp
from jax import lax
from jax.experimental import pallas as pl
from jax.experimental.pallas import tpu as pltpu
from jax.sharding import Mesh
from jax.sharding import PartitionSpec as P

DP = ("dp_0", "dp_1", "dp_2")
MESH = pl.DeviceIdType.MESH
EPSILON = 1e-05
Z, Y, X = 12, 8, 4
TOK, D, HD = 128, 8192, 128
ROWS = 43
CHUNK = 16 * ROWS
HALF, LIFT = 352, 336
FAR, FAR_STEP = 112, 80
OWN = 64
NEAR = (3, 9, 2, 10, 1, 11)
FARS = (4, 5, 6, 7, 8)
SHARE = D // X


def own_start(block):
    return lax.div(ROWS * block, 16) * 16


def kernel(
    hid_hbm, w_hbm, gk_hbm, gain_ref, cnt_ref, kg_ref, ng_hbm,
    hid, wbuf, heads, part, pair, summed, near, far, near_sum, far_sum, near_in, far_in, acc, ngv,
    cnt_own, cnt_in, cnt_mid, cnt_in2,
    hid_sem, loc_sem, out_sem,
    wx_s, wx_r, gx_s, gx_r, wf_s, wf_r, pair_s, pair_r, near_s, near_r, far_s, far_r,
    n2_s, n2_r, f2_s, f2_r, c1_s, c1_r, c2_s, c2_r,
):
    z = lax.axis_index("dp_0")
    y = lax.axis_index("dp_1")
    c = lax.axis_index("dp_2")
    x = lax.axis_index("tensor")
    half = lax.div(y, 4)
    at_z = lambda d: lax.rem(z + d, Z)
    at_y = lambda d: lax.rem(y + d, Y)

    def remote(src, dst, ss, rs, zz=None, yy=None, cc=None, xx=None):
        return pltpu.make_async_remote_copy(
            src_ref=src, dst_ref=dst, send_sem=ss, recv_sem=rs,
            device_id=(
                z if zz is None else zz,
                y if yy is None else yy,
                c if cc is None else cc,
                x if xx is None else xx,
            ),
            device_id_type=MESH,
        )

    loads = []
    for i in range(4):
        cols = pl.ds(i * SHARE, SHARE)
        load = pltpu.make_async_copy(hid_hbm.at[:, cols], hid.at[:, cols], hid_sem.at[i])
        load.start()
        loads.append(load)
    gk_load = pltpu.make_async_copy(gk_hbm, heads.at[0], loc_sem.at[0])
    gk_load.start()
    mine = pl.ds(pl.multiple_of(x * SHARE, SHARE), SHARE)
    w_load = pltpu.make_async_copy(w_hbm.at[mine, :], wbuf.at[0], loc_sem.at[1])
    w_load.start()

    barrier = pltpu.get_barrier_semaphore()

    def greet(zz, yy, cc, xx):
        pl.semaphore_signal(barrier, inc=1, device_id=(zz, yy, cc, xx), device_id_type=MESH)

    greet(z, y, 1 - c, x)
    for k in range(1, X):
        greet(z, y, c, lax.rem(x + k, X))
    for d in range(1, Y):
        greet(z, at_y(d), c, x)
        greet(z, at_y(d), 1 - c, x)
    for d in range(1, Z):
        greet(at_z(d), y, c, x)
    for d in FARS:
        greet(at_z(d), y, 1 - c, x)
    greeted = 1 + 3 + 14 + 11 + 5

    count = cnt_ref[0]
    cnt_own[...] = jnp.full((8, 128), count, jnp.int32).astype(jnp.float32)

    squares = jnp.zeros((TOK, 128), jnp.float32)
    for i in range(4):
        loads[i].wait()

        def add_squares(t, total, i=i):
            lanes = pl.ds(pl.multiple_of(i * SHARE + t * 128, 128), 128)
            v = hid[:, lanes].astype(jnp.float32)
            return total + v * v

        squares = lax.fori_loop(0, SHARE // 128, add_squares, squares, unroll=4)
    inv_rms = lax.rsqrt(jnp.sum(squares, axis=1, keepdims=True) * (1.0 / D) + EPSILON)
    live = lax.broadcasted_iota(jnp.int32, (TOK, HD), 0) < count
    gk_load.wait()
    scaled = jnp.where(live, heads[0].astype(jnp.float32) * inv_rms, 0.0).astype(jnp.bfloat16)

    pl.semaphore_wait(barrier, greeted)

    gx, wx = [], []
    for k in (2, 1, 3):
        xx = lax.rem(x + k, X)
        send = remote(gk_hbm, heads.at[k], gx_s.at[k - 1], gx_r.at[k - 1], xx=xx)
        send.start()
        gx.append(send)
    upper = pl.ds(pl.multiple_of(c * (SHARE // 2), SHARE // 2), SHARE // 2)
    for k in (1, 3, 2):
        xx = lax.rem(x + k, X)
        theirs = pl.ds(pl.multiple_of(xx * SHARE + c * (SHARE // 2), SHARE // 2), SHARE // 2)
        send = remote(
            w_hbm.at[theirs, :], wbuf.at[k, upper, :], wx_s.at[k - 1], wx_r.at[k - 1], xx=xx
        )
        send.start()
        wx.append((k, send))
    c1 = []
    for d in range(Y):
        for e in range(2):
            if d + e == 0:
                continue
            slot = 2 * d + e - 1
            send = remote(
                cnt_own, cnt_in.at[slot], c1_s.at[slot], c1_r.at[slot],
                yy=at_y(d), cc=c if e == 0 else 1 - c,
            )
            send.start()
            c1.append(send)

    BLOCK = 512

    def block_term(t, _):
        at = pl.multiple_of(t * BLOCK, BLOCK)
        term = lax.dot_general(
            hid[:, pl.ds(at, BLOCK)], scaled, (((0,), (0,)), ((), ())),
            preferred_element_type=jnp.float32,
        )
        part[pl.ds(at, BLOCK), :] = term.astype(jnp.bfloat16)
        return 0

    lax.fori_loop(0, D // BLOCK, block_term, 0)
    part[D:, :] = jnp.zeros((Z * CHUNK - D, HD), jnp.bfloat16)

    order = NEAR[:2] + FARS + NEAR[2:] + (0,)
    pairs = {}
    for j in order:
        rows = pl.ds(pl.multiple_of(at_z(j) * CHUNK + (1 - c) * LIFT, 16), HALF)
        pairs[j] = remote(
            part.at[rows, :], pair.at[j], pair_s.at[j], pair_r.at[j], cc=1 - c
        )
        pairs[j].start()
    near_sends, far_sends = [], []
    for j in order:
        pairs[j].wait_recv()
        rows = pl.ds(pl.multiple_of(at_z(j) * CHUNK + c * LIFT, 16), HALF)
        summed[j] = (
            part[rows, :].astype(jnp.float32) + pair[j].astype(jnp.float32)
        ).astype(jnp.bfloat16)
        if j in NEAR:
            n = NEAR.index(j)
            send = remote(summed.at[j], near.at[n], near_s.at[n], near_r.at[n], zz=at_z(j))
            send.start()
            near_sends.append(send)
        if j == FARS[-1]:
            for r in (4, 3, 5, 2, 6, 1, 7):
                yy = at_y(r)
                window = pl.ds(pl.multiple_of(lax.rem(yy, 4) * FAR_STEP, 16), FAR)
                send = remote(
                    summed.at[pl.ds(FARS[0], len(FARS)), window, :], far.at[r - 1],
                    far_s.at[r - 1], far_r.at[r - 1], yy=yy,
                )
                there = lax.div(yy, 4) == c
                pl.when(there)(send.start)
                far_sends.append((there, send))

    for send in c1:
        send.wait_recv()
    cnt_mid[...] = cnt_own[...] + jnp.sum(cnt_in[...], axis=0)
    c2 = []
    for d in range(1, Z):
        send = remote(cnt_mid, cnt_in2.at[d - 1], c2_s.at[d - 1], c2_r.at[d - 1], zz=at_z(d))
        send.start()
        c2.append(send)

    wf = []
    for k, send in wx:
        send.wait_recv()
        forward = remote(
            wbuf.at[k, upper, :], wbuf.at[k, upper, :], wf_s.at[k - 1], wf_r.at[k - 1], cc=1 - c
        )
        forward.start()
        wf.append(forward)

    for send in near_sends:
        send.wait_recv()

    def near_total(t, _):
        rows = pl.ds(pl.multiple_of(t * 32, 32), 32)
        total = summed[0, rows, :].astype(jnp.float32)
        for n in range(len(NEAR)):
            total = total + near[n, rows, :].astype(jnp.float32)
        near_sum[rows, :] = total.astype(jnp.bfloat16)
        return 0

    lax.fori_loop(0, HALF // 32, near_total, 0)
    n2 = []
    for r in (4, 3, 5, 2, 6, 1, 7, 0):
        yy = at_y(r)
        for e in range(2):
            window = pl.ds(pl.multiple_of(own_start(2 * lax.rem(yy, 4) + e), 16), OWN)
            send = remote(
                near_sum.at[window, :], near_in.at[r], n2_s.at[2 * r + e], n2_r.at[r], yy=yy, cc=e
            )
            there = lax.div(yy, 4) == c
            if r == 0:
                there = jnp.logical_and(there, c != e)
            pl.when(there)(send.start)
            n2.append((there, send))
    mine8 = 2 * lax.rem(y, 4) + c

    @pl.when(half == c)
    def _():
        near_in[0] = near_sum[pl.ds(pl.multiple_of(own_start(mine8), 16), OWN), :]

    f2 = []
    quarter = lax.rem(y, 4)
    for n, j in enumerate(FARS):
        for e in range(2):
            inside = own_start(2 * quarter + e) - FAR_STEP * quarter
            window = pl.ds(pl.multiple_of(inside, 16), OWN)
            f2.append(
                remote(
                    far_sum.at[n, window, :], far_in.at[n], f2_s.at[2 * n + e], f2_r.at[n],
                    zz=at_z(j), cc=e,
                )
            )

    @pl.when(half == c)
    def _():
        for r in range(1, Y):
            pltpu.make_async_copy(far.at[r - 1], far.at[r - 1], far_r.at[r - 1]).wait()
        start = pl.multiple_of(quarter * FAR_STEP, 16)
        for n, j in enumerate(FARS):
            total = summed[j, pl.ds(start, FAR), :].astype(jnp.float32)
            for r in range(1, Y):
                total = total + far[r - 1, n].astype(jnp.float32)
            far_sum[n] = total.astype(jnp.bfloat16)
            for e in range(2):
                f2[2 * n + e].start()

    for send in c2:
        send.wait_recv()
    weighting = (1.0 * TOK * Z * Y * 2) / (cnt_mid[...] + jnp.sum(cnt_in2[...], axis=0))
    weight = weighting[0:1, 0:1]
    w_load.wait()
    for send in gx:
        send.wait_recv()
    for forward in wf:
        forward.wait_recv()
    for k in range(X):
        heads[k] = jnp.where(live, heads[k].astype(jnp.float32), 0.0).astype(jnp.bfloat16)
    TILE = 512
    outs = []
    for t in range(SHARE // TILE):
        cols = pl.ds(t * TILE, TILE)
        total = None
        for k in range(X):
            term = lax.dot_general(
                heads[k], wbuf[k, cols, :], (((1,), (1,)), ((), ())),
                preferred_element_type=jnp.float32,
            )
            total = term if total is None else total + term
        ngv[:, cols] = (total * weight).astype(jnp.bfloat16)
        out = pltpu.make_async_copy(ngv.at[:, cols], ng_hbm.at[:, cols], out_sem.at[t])
        out.start()
        outs.append(out)

    first = ROWS * ((z * Y + y) * 2 + c)
    shift = ROWS * mine8 + 8 * half - own_start(mine8)
    feature = first + lax.broadcasted_iota(jnp.int32, (48, 128), 0)
    lane = lax.broadcasted_iota(jnp.int32, (48, 128), 1)
    line = lax.div(first, 128)
    gains = jnp.zeros((48, 128), jnp.float32)
    for n in range(2):
        at = jnp.minimum(line + n, D // 128 - 1)
        row = gain_ref[pl.ds(at, 1), :]
        gains = jnp.where(feature == at * 128 + lane, row, gains)
    gain_rows = jnp.sum(gains, axis=1, keepdims=True)

    for r in range(1, Y):
        pltpu.make_async_copy(near_in.at[r], near_in.at[r], n2_r.at[r]).wait()

    @pl.when(half != c)
    def _():
        pltpu.make_async_copy(near_in.at[0], near_in.at[0], n2_r.at[0]).wait()

    for n in range(len(FARS)):
        pltpu.make_async_copy(far_in.at[n], far_in.at[n], f2_r.at[n]).wait()
    total = near_in[0].astype(jnp.float32)
    for r in range(1, Y):
        total = total + near_in[r].astype(jnp.float32)
    for n in range(len(FARS)):
        total = total + far_in[n].astype(jnp.float32)
    acc[0:OWN, :] = total
    own = acc[pl.ds(shift, 48), :] * (gain_rows * weight)
    kg_ref[...] = own[0:ROWS, :]

    for send in [*gx, *[s for _, s in wx], *c1, *wf, *pairs.values(), *near_sends, *c2]:
        send.wait_send()
    for there, send in [*far_sends, *n2]:
        pl.when(there)(send.wait_send)

    @pl.when(half == c)
    def _():
        for send in f2:
            send.wait_send()

    for out in outs:
        out.wait()


def fused(hidden, w_key, grad_key, gain, counts):
    bf16, f32 = jnp.bfloat16, jnp.float32
    dma = pltpu.SemaphoreType.DMA
    hbm = pl.BlockSpec(memory_space=pl.ANY)
    vmem = pl.BlockSpec(memory_space=pltpu.VMEM)
    return pl.pallas_call(
        kernel,
        out_shape=(
            jax.ShapeDtypeStruct((ROWS, HD), f32),
            jax.ShapeDtypeStruct((TOK, SHARE), bf16),
        ),
        in_specs=[hbm, hbm, hbm, vmem, pl.BlockSpec(memory_space=pltpu.SMEM)],
        out_specs=(vmem, hbm),
        scratch_shapes=[
            pltpu.VMEM((TOK, D), bf16),
            pltpu.VMEM((X, SHARE, HD), bf16),
            pltpu.VMEM((X, TOK, HD), bf16),
            pltpu.VMEM((Z * CHUNK, HD), bf16),
            pltpu.VMEM((Z, HALF, HD), bf16),
            pltpu.VMEM((Z, HALF, HD), bf16),
            pltpu.VMEM((len(NEAR), HALF, HD), bf16),
            pltpu.VMEM((Y - 1, len(FARS), FAR, HD), bf16),
            pltpu.VMEM((HALF, HD), bf16),
            pltpu.VMEM((len(FARS), FAR, HD), bf16),
            pltpu.VMEM((Y, OWN, HD), bf16),
            pltpu.VMEM((len(FARS), OWN, HD), bf16),
            pltpu.VMEM((OWN + 16, HD), f32),
            pltpu.VMEM((TOK, SHARE), bf16),
            pltpu.VMEM((8, 128), f32),
            pltpu.VMEM((15, 8, 128), f32),
            pltpu.VMEM((8, 128), f32),
            pltpu.VMEM((11, 8, 128), f32),
            dma((4,)), dma((2,)), dma((4,)),
            dma((3,)), dma((3,)), dma((3,)), dma((3,)), dma((3,)), dma((3,)),
            dma((Z,)), dma((Z,)), dma((6,)), dma((6,)), dma((7,)), dma((7,)),
            dma((16,)), dma((8,)), dma((10,)), dma((5,)), dma((15,)), dma((15,)),
            dma((11,)), dma((11,)),
        ],
        compiler_params=pltpu.CompilerParams(collective_id=0, has_side_effects=True),
    )(hidden, w_key, grad_key, gain, counts)


def per_device(hidden, gain, w_key, grad_key, counts):
    return fused(hidden, w_key, grad_key, gain.reshape(D // 128, 128), counts)


def solution(mesh):
    split = Mesh(
        mesh.devices.reshape(Z, Y, 2, mesh.shape["tensor"]), ("dp_0", "dp_1", "dp_2", "tensor")
    )
    return jax.shard_map(
        per_device,
        mesh=split,
        in_specs=(P(DP, None), P(), P(None, "tensor"), P(DP, "tensor"), P(DP)),
        out_specs=(P(DP, "tensor"), P(DP, "tensor")),
        check_vma=False,
    )
```

time: 355 us -> 56 us (0.16)
  waiting for transfers between devices: 249 us -> 0 us
  blocking collectives: 56.5 us -> 0 us
  Pallas kernels: 0 us -> 51.2 us
  between operations: 15.6 us -> 1.29 us
  local copies, waits for them, and re-layouts: 16.7 us -> 3.23 us
  other arithmetic: 7.86 us -> 0 us
  starting transfers between devices: 4.86 us -> 0 us
    reduce_scatter x1 -> x0, waiting for transfers between devices: 249 us -> none  [own_tiles(): own = lax.psum_scatter(lines, axis, scatter_dimension=0, tiled=True)]
    psum x3 -> x0, blocking collectives: 56.5 us -> none  [one_axis_at_a_time(): return functools.reduce(lax.psum, axes, x)]
    pallas_call x0 -> x1, Pallas kernels: none -> 51.2 us  [fused(): pl.pallas_call(kernel, out_shape=(jax.ShapeDtypeStruct((ROWS, HD), f32),...]
    reshape x2 -> x0, local copies, waits for them, and re-layouts: 6.71 us -> none  [the longest x1 5.19 us: own_tiles(): jnp.pad(lines, ((0, 0), (0, span * 128 - lines.shape[1]))).reshape(-1, 128)]
    another operation x1 -> x0, local copies, waits for them, and re-layouts: 5.02 us -> none  [own_tiles(): lines = tiles.reshape(devices, -1)]
    pad x1 -> x0, local copies, waits for them, and re-layouts: 4.9 us -> none  [own_tiles(): jnp.pad(lines, ((0, 0), (0, span * 128 - lines.shape[1]))).reshape(-1, 128)]
    all_to_all x1 -> x0, starting transfers between devices: 4.83 us -> none  [sent_and_summed(): tiles = lax.all_to_all(cut_along(x, dim, devices), axis, 0, 0, tiled=True)]
    reduce_sum x2 -> x0, other arithmetic: 4.3 us -> none  [the longest x1 2.18 us: per_device(): jnp.mean(wide_hidden * wide_hidden, axis=1, keepdims=True) + EPSILON]
  transfers between devices with their start and end apart: 2 -> 0, of which waited for: 1 -> 0; matrix products, arithmetic and copies ran while one was open for 1% -> 0% of each run, Pallas kernels for 0% -> 0%
where the time goes in v1:
time: 56 us; the launch traced here: 55.7 us
  Pallas kernels  51.2 us (91%)
  local copies, waits for them, and re-layouts  3.23 us (6%)
  between operations  1.29 us (2%)
    pallas_call x1, Pallas kernels, fused(): pl.pallas_call(kernel, out_shape=(jax.ShapeDtypeStruct((ROWS, HD), f32),...  51.2 us
    unnamed x2, local copies, waits for them, and re-layouts  3.23 us

profile of v1, /device:TPU:1, one launch (start us, length us, event | category | flops | bytes accessed | tf_op | source)
XLA Modules:
  0.0 55.7 jit_solution(14136849632563300904)
XLA Ops:
  1.3 51.2 %shard_map.68 = (f32[43,128]{1,0:T(8,128)}, bf16[128,2048]{1,0:T(8,128)(2,1)}) custom-call(bf16[128,8192]{1,0:T(8,128)(2,1)} %hid_hbm.1, bf16[8192,128]{1,0:T(8,128)(2,1)} %w_hbm.1, bf16[128,128]{1,0:T(8,128)(2,1)} %gk_hbm.1, f32[64,128]{1,0:T(8,128)} %bitcast.1, s32[1]{0:T(128)S(6)} %copy.9.cnt_ref), custom_call_target="tpu_custom_call" | custom-call | tf_op jit(solution)/shard_map/pallas_call | solution.py:332
  52.5 1.3 %copy.10 = f32[43,128]{1,0:T(8,128)} copy(f32[43,128]{1,0:T(8,128)} %get-tuple-element.4) | data formatting | bytes 44032
  53.8 1.9 %copy.11 = bf16[128,2048]{1,0:T(8,128)(2,1)} copy(bf16[128,2048]{1,0:T(8,128)(2,1)} %get-tuple-element.5) | data formatting | bytes 1048576

commit v2 on v1

--- a/solution.py
+++ b/solution.py
@@ -28,8 +28,8 @@
 
 
 def kernel(
-    hid_hbm, w_hbm, gk_hbm, gain_ref, cnt_ref, kg_ref, ng_hbm,
-    hid, wbuf, heads, part, pair, summed, near, far, near_sum, far_sum, near_in, far_in, acc, ngv,
+    hid_hbm, w_hbm, gk_hbm, gain_hbm, cnt_hbm, kg_ref, ng_hbm,
+    gain_ref, cnt_ref, hid, turned, wbuf, heads, part, pair, summed, near, far, near_sum, far_sum, near_in, far_in, acc, ngv,
     cnt_own, cnt_in, cnt_mid, cnt_in2,
     hid_sem, loc_sem, out_sem,
     wx_s, wx_r, gx_s, gx_r, wf_s, wf_r, pair_s, pair_r, near_s, near_r, far_s, far_r,
@@ -63,6 +63,10 @@
         loads.append(load)
     gk_load = pltpu.make_async_copy(gk_hbm, heads.at[0], loc_sem.at[0])
     gk_load.start()
+    cnt_load = pltpu.make_async_copy(cnt_hbm, cnt_ref, loc_sem.at[2])
+    cnt_load.start()
+    gain_load = pltpu.make_async_copy(gain_hbm, gain_ref, loc_sem.at[3])
+    gain_load.start()
     mine = pl.ds(pl.multiple_of(x * SHARE, SHARE), SHARE)
     w_load = pltpu.make_async_copy(w_hbm.at[mine, :], wbuf.at[0], loc_sem.at[1])
     w_load.start()
@@ -84,6 +88,7 @@
         greet(at_z(d), y, 1 - c, x)
     greeted = 1 + 3 + 14 + 11 + 5
 
+    cnt_load.wait()
     count = cnt_ref[0]
     cnt_own[...] = jnp.full((8, 128), count, jnp.int32).astype(jnp.float32)
 
@@ -93,7 +98,9 @@
 
         def add_squares(t, total, i=i):
             lanes = pl.ds(pl.multiple_of(i * SHARE + t * 128, 128), 128)
-            v = hid[:, lanes].astype(jnp.float32)
+            block = hid[:, lanes]
+            turned[lanes, :] = block.T
+            v = block.astype(jnp.float32)
             return total + v * v
 
         squares = lax.fori_loop(0, SHARE // 128, add_squares, squares, unroll=4)
@@ -101,6 +108,17 @@
     live = lax.broadcasted_iota(jnp.int32, (TOK, HD), 0) < count
     gk_load.wait()
     scaled = jnp.where(live, heads[0].astype(jnp.float32) * inv_rms, 0.0).astype(jnp.bfloat16)
+
+    BLOCK = 512
+
+    def block_term(t, _):
+        at = pl.multiple_of(t * BLOCK, BLOCK)
+        term = jnp.dot(turned[pl.ds(at, BLOCK), :], scaled, preferred_element_type=jnp.float32)
+        part[pl.ds(at, BLOCK), :] = term.astype(jnp.bfloat16)
+        return 0
+
+    lax.fori_loop(0, D // BLOCK, block_term, 0, unroll=2)
+    part[D:, :] = jnp.zeros((Z * CHUNK - D, HD), jnp.bfloat16)
 
     pl.semaphore_wait(barrier, greeted)
 
@@ -131,20 +149,6 @@
             )
             send.start()
             c1.append(send)
-
-    BLOCK = 512
-
-    def block_term(t, _):
-        at = pl.multiple_of(t * BLOCK, BLOCK)
-        term = lax.dot_general(
-            hid[:, pl.ds(at, BLOCK)], scaled, (((0,), (0,)), ((), ())),
-            preferred_element_type=jnp.float32,
-        )
-        part[pl.ds(at, BLOCK), :] = term.astype(jnp.bfloat16)
-        return 0
-
-    lax.fori_loop(0, D // BLOCK, block_term, 0)
-    part[D:, :] = jnp.zeros((Z * CHUNK - D, HD), jnp.bfloat16)
 
     order = NEAR[:2] + FARS + NEAR[2:] + (0,)
     pairs = {}
@@ -280,6 +284,7 @@
         out.start()
         outs.append(out)
 
+    gain_load.wait()
     first = ROWS * ((z * Y + y) * 2 + c)
     shift = ROWS * mine8 + 8 * half - own_start(mine8)
     feature = first + lax.broadcasted_iota(jnp.int32, (48, 128), 0)
@@ -327,7 +332,8 @@
 def fused(hidden, w_key, grad_key, gain, counts):
     bf16, f32 = jnp.bfloat16, jnp.float32
     dma = pltpu.SemaphoreType.DMA
-    hbm = pl.BlockSpec(memory_space=pl.ANY)
+    hbm = pl.BlockSpec(memory_space=pltpu.HBM)
+    anywhere = pl.BlockSpec(memory_space=pl.ANY)
     vmem = pl.BlockSpec(memory_space=pltpu.VMEM)
     return pl.pallas_call(
         kernel,
@@ -335,10 +341,13 @@
             jax.ShapeDtypeStruct((ROWS, HD), f32),
             jax.ShapeDtypeStruct((TOK, SHARE), bf16),
         ),
-        in_specs=[hbm, hbm, hbm, vmem, pl.BlockSpec(memory_space=pltpu.SMEM)],
-        out_specs=(vmem, hbm),
+        in_specs=[hbm] * 5,
+        out_specs=(vmem, anywhere),
         scratch_shapes=[
+            pltpu.VMEM((D // 128, 128), f32),
+            pltpu.SMEM((1,), jnp.int32),
             pltpu.VMEM((TOK, D), bf16),
+            pltpu.VMEM((D, TOK), bf16),
             pltpu.VMEM((X, SHARE, HD), bf16),
             pltpu.VMEM((X, TOK, HD), bf16),
             pltpu.VMEM((Z * CHUNK, HD), bf16),
@@ -356,18 +365,20 @@
             pltpu.VMEM((15, 8, 128), f32),
             pltpu.VMEM((8, 128), f32),
             pltpu.VMEM((11, 8, 128), f32),
-            dma((4,)), dma((2,)), dma((4,)),
+            dma((4,)), dma((4,)), dma((4,)),
             dma((3,)), dma((3,)), dma((3,)), dma((3,)), dma((3,)), dma((3,)),
             dma((Z,)), dma((Z,)), dma((6,)), dma((6,)), dma((7,)), dma((7,)),
             dma((16,)), dma((8,)), dma((10,)), dma((5,)), dma((15,)), dma((15,)),
             dma((11,)), dma((11,)),
         ],
-        compiler_params=pltpu.CompilerParams(collective_id=0, has_side_effects=True),
+        compiler_params=pltpu.CompilerParams(collective_id=0, has_side_effects=True, vmem_limit_bytes=24 << 20),
     )(hidden, w_key, grad_key, gain, counts)
 
 
 def per_device(hidden, gain, w_key, grad_key, counts):
-    return fused(hidden, w_key, grad_key, gain.reshape(D // 128, 128), counts)
+    in_hbm = lambda v: pltpu.with_memory_space_constraint(v, pltpu.HBM)
+    gain = gain.reshape(D // 128, 128)
+    return fused(*(in_hbm(v) for v in (hidden, w_key, grad_key, gain)), counts)
 
 
 def solution(mesh):

time: 56 us -> 49.7 us (0.89)
  Pallas kernels: 51.2 us -> 46.8 us
  local copies, waits for them, and re-layouts: 3.23 us -> 1.4 us
    pallas_call x1, Pallas kernels: 51.2 us -> 46.8 us  [fused(): pl.pallas_call(kernel, out_shape=(jax.ShapeDtypeStruct((ROWS, HD), f32),...]
    unnamed x2, local copies, waits for them, and re-layouts: 3.23 us -> 1.4 us
where the time goes in v2:
time: 49.7 us; the launch traced here: 49.5 us
  Pallas kernels  46.8 us (94%)
  local copies, waits for them, and re-layouts  1.4 us (3%)
  between operations  1.29 us (3%)
    pallas_call x1, Pallas kernels, fused(): pl.pallas_call(kernel, out_shape=(jax.ShapeDtypeStruct((ROWS, HD), f32),...  46.8 us
    unnamed x2, local copies, waits for them, and re-layouts  1.4 us

profile of v2, /device:TPU:1, one launch (start us, length us, event | category | flops | bytes accessed | tf_op | source)
XLA Modules:
  0.0 49.5 jit_solution(11442527071190916786)
XLA Ops:
  1.3 46.8 %shard_map.68 = (f32[43,128]{1,0:T(8,128)S(1)}, bf16[128,2048]{1,0:T(8,128)(2,1)S(1)}) custom-call(bf16[128,8192]{1,0:T(8,128)(2,1)} %hid_hbm.1, bf16[8192,128]{1,0:T(8,128)(2,1)} %w_hbm.1, bf16[128,128]{1,0:T(8,128)(2,1)} %gk_hbm.1, f32[64,128]{1,0:T(8,128)} %bitcast.1, s32[1]{0:T(128)S(6)} %copy.9.cnt_hbm), custom_call_target="tpu_custom_call" | custom-call | tf_op jit(solution)/shard_map/pallas_call | solution.py:338
  48.1 0.6 %copy.10 = f32[43,128]{1,0:T(8,128)} copy(f32[43,128]{1,0:T(8,128)S(1)} %get-tuple-element.4) | data formatting | bytes 44032
  48.7 0.8 %copy.11 = bf16[128,2048]{1,0:T(8,128)(2,1)} copy(bf16[128,2048]{1,0:T(8,128)(2,1)S(1)} %get-tuple-element.5) | data formatting | bytes 1048576

commit v3 on v0

v3 whole, which is shorter than its diff:
```python
import jax
import jax.numpy as jnp
from jax import lax
from jax.experimental import pallas as pl
from jax.experimental.pallas import tpu as pltpu
from jax.sharding import Mesh
from jax.sharding import PartitionSpec as P

DP = ("dp_0", "dp_1", "dp_2")
MESH = pl.DeviceIdType.MESH
EPSILON = 1e-05
Z, Y, X = 12, 8, 4
TOK, D, HD = 128, 8192, 128
ROWS = 43
CHUNK = 16 * ROWS
HALF, LIFT = 352, 336
LEAD = 4
FAR = 96
OWN = 48
FARS = (6, 5, 7, 4, 8)
PARTS = ((0, 2, 1), (2, 5, -1))
GROUPS = (FARS[:2], FARS[2:], (3, 9), (1, 11, 2, 10, 0))
NF = len(FARS)
SHARE = D // X


def kernel(
    hid_hbm, w_hbm, gk_hbm, gain_hbm, cnt_hbm, kg_ref, ng_hbm,
    gain_ref, cnt_ref, hid, turned, wbuf, heads, scaled, other, pair, shifted, summed, sumfar,
    near_mid, near_out, near, far_mid, far_out, far,
    near_f, near_own, far_f, far_own, near_in, far_in, ngv,
    cnt_own, cnt_in, cnt_mid, cnt_in2,
    hid_sem, loc_sem, out_sem,
    wx_s, wx_r, gx_s, gx_r, wf_s, wf_r, pair_s, pair_r, near_s, near_r, far_s, far_r,
    n2_s, n2_r, f2_s, f2_r, c1_s, c1_r, c2_s, c2_r,
):
    z = lax.axis_index("dp_0")
    y = lax.axis_index("dp_1")
    c = lax.axis_index("dp_2")
    x = lax.axis_index("tensor")
    half, quarter = lax.div(y, 4), lax.rem(y, 4)
    at_z = lambda d: lax.rem(z + d, Z)
    at_y = lambda d: lax.rem(y + d, Y)
    f32, bf16 = jnp.float32, jnp.bfloat16

    def remote(src, dst, ss, rs, zz=None, yy=None, cc=None, xx=None):
        return pltpu.make_async_remote_copy(
            src_ref=src, dst_ref=dst, send_sem=ss, recv_sem=rs,
            device_id=(
                z if zz is None else zz,
                y if yy is None else yy,
                c if cc is None else cc,
                x if xx is None else xx,
            ),
            device_id_type=MESH,
        )

    PIECES = 8
    loads = []
    for i in range(PIECES):
        cols = pl.ds(i * (D // PIECES), D // PIECES)
        load = pltpu.make_async_copy(hid_hbm.at[:, cols], hid.at[:, cols], hid_sem.at[i])
        load.start()
        loads.append(load)
    cnt_load = pltpu.make_async_copy(cnt_hbm, cnt_ref, loc_sem.at[2])
    cnt_load.start()
    gk_load = pltpu.make_async_copy(gk_hbm, heads.at[0], loc_sem.at[0])
    gk_load.start()
    gain_load = pltpu.make_async_copy(gain_hbm, gain_ref, loc_sem.at[3])
    gain_load.start()
    mine = pl.ds(pl.multiple_of(x * SHARE, SHARE), SHARE)
    w_load = pltpu.make_async_copy(w_hbm.at[mine, :], wbuf.at[0], loc_sem.at[1])
    w_load.start()

    barrier = pltpu.get_barrier_semaphore()

    def greet(zz, yy, cc, xx):
        pl.semaphore_signal(barrier, inc=1, device_id=(zz, yy, cc, xx), device_id_type=MESH)

    for d in (6, 5, 7, 4, 8, 3, 9, 2, 10, 1, 11):
        greet(at_z(d), y, c, x)
        if d in FARS:
            greet(at_z(d), y, 1 - c, x)
    for d in (4, 3, 5, 2, 6, 1, 7):
        greet(z, at_y(d), c, x)
        greet(z, at_y(d), 1 - c, x)
    for k in range(1, X):
        greet(z, y, c, lax.rem(x + k, X))
    greet(z, y, 1 - c, x)
    greeted = 1 + 3 + 14 + 11 + NF

    cnt_load.wait()
    count = cnt_ref[0]
    cnt_own[...] = jnp.full((8, 128), count, jnp.int32).astype(f32)
    turned[D:, :] = jnp.zeros((Z * CHUNK - D, TOK), bf16)
    for s in range(NF):
        shifted[s, 0:8, :] = jnp.zeros((8, 128), f32)
        shifted[s, HALF + 8 :, :] = jnp.zeros((8, 128), f32)

    squares = jnp.zeros((TOK, 128), f32)
    for i in range(PIECES):
        loads[i].wait()

        def add_squares(t, total, i=i):
            lanes = pl.ds(pl.multiple_of(i * (D // PIECES) + t * 128, 128), 128)
            block = hid[:, lanes]
            turned[lanes, :] = block.T
            v = block.astype(f32)
            return total + v * v

        squares = lax.fori_loop(0, D // PIECES // 128, add_squares, squares, unroll=4)
    inv_rms = lax.rsqrt(jnp.sum(squares, axis=1, keepdims=True) * (1.0 / D) + EPSILON)
    live = lax.broadcasted_iota(jnp.int32, (TOK, HD), 0) < count
    gk_load.wait()
    scaled[...] = jnp.where(live, heads[0].astype(f32) * inv_rms, 0.0).astype(bf16)

    pl.semaphore_wait(barrier, greeted)

    near_sends, far_sends = {}, []
    pairs, gx, wx, c1 = {}, [], [], []
    upper = pl.ds(pl.multiple_of(c * (SHARE // 2), SHARE // 2), SHARE // 2)

    def window(target):
        start = lax.div(LEAD + 2 * ROWS * lax.rem(target, 4), 16) * 16
        return pl.ds(pl.multiple_of(start, 16), FAR)

    def here(r):
        return lax.div(at_y(r), 4) == c

    def mine_far(r, first, last):
        return sumfar.at[pl.ds(first, last - first), window(at_y(r)), :]

    def share(j):
        theirs = pl.multiple_of(at_z(j) * CHUNK + (1 - c) * LIFT, 16)
        pairs[j] = remote(
            turned.at[pl.ds(theirs, HALF), :], pair.at[j], pair_s.at[j], pair_r.at[j], cc=1 - c
        )
        pairs[j].start()

    def weights_along_x():
        for k in (1, 3, 2):
            xx = lax.rem(x + k, X)
            theirs = pl.ds(pl.multiple_of(xx * SHARE + c * (SHARE // 2), SHARE // 2), SHARE // 2)
            send = remote(
                w_hbm.at[theirs, :], wbuf.at[k, upper, :], wx_s.at[k - 1], wx_r.at[k - 1], xx=xx
            )
            send.start()
            wx.append((k, send))
        for k in (2, 1, 3):
            xx = lax.rem(x + k, X)
            send = remote(gk_hbm, heads.at[k], gx_s.at[k - 1], gx_r.at[k - 1], xx=xx)
            send.start()
            gx.append(send)

    def counts_along_y():
        for d in range(Y):
            for e in range(2):
                if d + e == 0:
                    continue
                slot = 2 * d + e - 1
                send = remote(
                    cnt_own, cnt_in.at[slot], c1_s.at[slot], c1_r.at[slot],
                    yy=at_y(d), cc=c if e == 0 else 1 - c,
                )
                send.start()
                c1.append(send)

    def send_near(i, src, dst, step):
        near_sends[i] = remote(src, dst, near_s.at[i], near_r.at[i], zz=at_z(step))
        near_sends[i].start()

    def send_far(i, src, dst, r, step):
        send = remote(src, dst, far_s.at[i], far_r.at[i], yy=at_y(step))
        pl.when(here(r))(send.start)
        far_sends.append((here(r), send))

    def finish(group, both):
        tokens = []
        for j in group:
            pairs[j].wait_recv()
            rows = pl.ds(pl.multiple_of(at_z(j) * CHUNK + c * LIFT, 16), HALF)
            tokens.append(jnp.concatenate([turned[rows, :], pair[j]], axis=1))
        total = jnp.dot(jnp.concatenate(tokens, axis=0), both, preferred_element_type=f32)
        for n, j in enumerate(group):
            one = total[n * HALF : (n + 1) * HALF]
            if j in FARS:
                i = FARS.index(j)
                shifted[i, 8 : HALF + 8, :] = one
                sumfar[i] = shifted[i, pl.ds(8 - LEAD + 8 * c, HALF), :].astype(bf16)
            else:
                summed[j] = one.astype(bf16)

    swap = remote(scaled, other, pair_s.at[Z], pair_r.at[Z], cc=1 - c)
    swap.start()
    pairs[Z] = swap
    for group in GROUPS:
        for j in group:
            share(j)
    weights_along_x()
    counts_along_y()
    swap.wait_recv()
    both = jnp.concatenate([scaled[...], other[...]], axis=0)
    def first_far(p):
        first, last, way = PARTS[p]
        n = pl.ds(first, last - first)
        for i, (r, dst, step) in enumerate(
            (
                (4, far_mid.at[0, n], way),
                (-3 * way, far_mid.at[1, n], -way),
                (2 * way, far_mid.at[2, n], way),
                (-way, far.at[0, n], -way),
            )
        ):
            send_far(7 * p + i, mine_far(r % Y, first, last), dst, r % Y, step % Y)

    finish(GROUPS[0], both)
    first_far(0)
    finish(GROUPS[1], both)
    first_far(1)
    finish(GROUPS[2], both)
    send_near(0, summed.at[3], near_mid.at[0], 1)
    send_near(1, summed.at[9], near_mid.at[1], 11)
    finish(GROUPS[3], both)
    send_near(2, summed.at[1], near.at[0], 1)
    send_near(3, summed.at[11], near.at[1], 11)

    for p, (first, last, way) in enumerate(PARTS):
        n = pl.ds(first, last - first)
        for m, r in enumerate((3 * way % Y, -2 * way % Y, way % Y)):

            @pl.when(here(r))
            def _(p=p, n=n, m=m, r=r, first=first, last=last):
                mid = far_mid.at[m, n]
                pltpu.make_async_copy(mid, mid, far_r.at[7 * p + m]).wait()
                rows = window(at_y(r))
                for i in range(first, last):
                    far_out[m, i] = sumfar[i, rows, :] + far_mid[m, i]

            send_far(7 * p + 4 + m, far_out.at[m, n], far.at[1 + m, n], r, r)

    for n, (j, step) in enumerate(((2, 2), (10, 10))):
        near_sends[n].wait_recv()

        def merge_near(t, _, n=n, j=j):
            rows = pl.ds(pl.multiple_of(t * 32, 32), 32)
            near_out[n, rows, :] = summed[j, rows, :] + near_mid[n, rows, :]
            return 0

        lax.fori_loop(0, HALF // 32, merge_near, 0, unroll=True)
        send_near(4 + n, near_out.at[n], near.at[2 + n], step)

    for send in c1:
        send.wait_recv()
    cnt_mid[...] = cnt_own[...] + jnp.sum(cnt_in[...], axis=0)
    c2 = []
    for d in range(1, Z):
        send = remote(cnt_mid, cnt_in2.at[d - 1], c2_s.at[d - 1], c2_r.at[d - 1], zz=at_z(d))
        send.start()
        c2.append(send)

    f2 = []
    for i, j in enumerate(FARS):
        for e in range(2):
            f2.append(
                remote(
                    far_own.at[i, e], far_in.at[i], f2_s.at[2 * i + e], f2_r.at[i],
                    zz=at_z(j), cc=e,
                )
            )

    @pl.when(half == c)
    def _():
        rows = window(y)
        start = LEAD + 2 * ROWS * quarter
        inside = start - lax.div(start, 16) * 16
        for p, (first, last, way) in enumerate(PARTS):
            n = pl.ds(first, last - first)
            for slot in range(4):
                come = far.at[slot, n]
                pltpu.make_async_copy(come, come, far_r.at[7 * p + 3 + slot]).wait()
            for i in range(first, last):
                total = sumfar[i, rows, :].astype(f32)
                for slot in range(4):
                    total = total + far[slot, i].astype(f32)
                far_f[i, 0:FAR, :] = total
                for e in range(2):
                    far_own[i, e] = far_f[i, pl.ds(inside + e * ROWS, OWN), :].astype(bf16)
                    f2[2 * i + e].start()

    for i in (2, 3, 4, 5):
        near_sends[i].wait_recv()

    def near_total(t, _):
        rows = pl.ds(pl.multiple_of(t * 32, 32), 32)
        total = summed[0, rows, :].astype(f32)
        for n in range(4):
            total = total + near[n, rows, :].astype(f32)
        near_f[rows, :] = total
        return 0

    lax.fori_loop(0, HALF // 32, near_total, 0, unroll=True)
    for b in range(8):
        near_own[b] = near_f[pl.ds(8 * c + ROWS * b, OWN), :].astype(bf16)
    n2 = []
    for r in (4, 3, 5, 2, 6, 1, 7, 0):
        yy = at_y(r)
        for e in range(2):
            send = remote(
                near_own.at[2 * lax.rem(yy, 4) + e], near_in.at[r], n2_s.at[2 * r + e],
                n2_r.at[r], yy=yy, cc=e,
            )
            there = here(r)
            if r == 0:
                there = jnp.logical_and(there, c != e)
            pl.when(there)(send.start)
            n2.append((there, send))

    @pl.when(half == c)
    def _():
        near_in[0] = near_own[2 * quarter + c]

    wf = []
    for k, send in wx:
        send.wait_recv()
        forward = remote(
            wbuf.at[k, upper, :], wbuf.at[k, upper, :], wf_s.at[k - 1], wf_r.at[k - 1], cc=1 - c
        )
        forward.start()
        wf.append(forward)

    gain_load.wait()
    first = ROWS * ((z * Y + y) * 2 + c)
    feature = first + lax.broadcasted_iota(jnp.int32, (OWN, 128), 0)
    lane = lax.broadcasted_iota(jnp.int32, (OWN, 128), 1)
    line = lax.div(first, 128)
    gains = jnp.zeros((OWN, 128), f32)
    for n in range(2):
        at = jnp.minimum(line + n, D // 128 - 1)
        row = gain_ref[pl.ds(at, 1), :]
        gains = jnp.where(feature == at * 128 + lane, row, gains)
    gain_rows = jnp.sum(gains, axis=1, keepdims=True)

    w_load.wait()
    for send in gx:
        send.wait_recv()
    for k in range(X):
        heads[k] = jnp.where(live, heads[k].astype(f32), 0.0).astype(bf16)
    for send in c2:
        send.wait_recv()
    weighting = (1.0 * TOK * Z * Y * 2) / (cnt_mid[...] + jnp.sum(cnt_in2[...], axis=0))
    weight = weighting[0:1, 0:1]
    TILE = 512
    outs = []
    for t in range(SHARE // TILE):
        if 2 * t == SHARE // TILE:
            for forward in wf:
                forward.wait_recv()
        first_half = 2 * t < SHARE // TILE
        base = (c if first_half else 1 - c) * (SHARE // 2) + (t % (SHARE // TILE // 2)) * TILE
        cols = pl.ds(pl.multiple_of(base, TILE), TILE)
        total = None
        for k in range(X):
            term = lax.dot_general(
                heads[k], wbuf[k, cols, :], (((1,), (1,)), ((), ())),
                preferred_element_type=f32,
            )
            total = term if total is None else total + term
        ngv[:, cols] = (total * weight).astype(bf16)
        out = pltpu.make_async_copy(ngv.at[:, cols], ng_hbm.at[:, cols], out_sem.at[t])
        out.start()
        outs.append(out)

    for r in range(1, Y):
        pltpu.make_async_copy(near_in.at[r], near_in.at[r], n2_r.at[r]).wait()

    @pl.when(half != c)
    def _():
        pltpu.make_async_copy(near_in.at[0], near_in.at[0], n2_r.at[0]).wait()

    total = near_in[0].astype(f32)
    for r in range(1, Y):
        total = total + near_in[r].astype(f32)
    for i in range(NF):
        pltpu.make_async_copy(far_in.at[i], far_in.at[i], f2_r.at[i]).wait()
    for i in range(NF):
        total = total + far_in[i].astype(f32)
    kg_ref[...] = (total * (gain_rows * weight))[0:ROWS, :]

    for send in [*gx, *[s for _, s in wx], *c1, *wf, *pairs.values(), *near_sends.values(), *c2]:
        send.wait_send()
    for there, send in [*far_sends, *n2]:
        pl.when(there)(send.wait_send)

    @pl.when(half == c)
    def _():
        for send in f2:
            send.wait_send()

    for out in outs:
        out.wait()


def fused(hidden, w_key, grad_key, gain, counts):
    bf16, f32 = jnp.bfloat16, jnp.float32
    dma = pltpu.SemaphoreType.DMA
    hbm = pl.BlockSpec(memory_space=pltpu.HBM)
    anywhere = pl.BlockSpec(memory_space=pl.ANY)
    return pl.pallas_call(
        kernel,
        out_shape=(
            jax.ShapeDtypeStruct((ROWS, HD), f32),
            jax.ShapeDtypeStruct((TOK, SHARE), bf16),
        ),
        in_specs=[hbm] * 5,
        out_specs=(pl.BlockSpec(memory_space=pltpu.VMEM), anywhere),
        scratch_shapes=[
            pltpu.VMEM((D // 128, 128), f32),
            pltpu.SMEM((1,), jnp.int32),
            pltpu.VMEM((TOK, D), bf16),
            pltpu.VMEM((Z * CHUNK, TOK), bf16),
            pltpu.VMEM((X, SHARE, HD), bf16),
            pltpu.VMEM((X, TOK, HD), bf16),
            pltpu.VMEM((TOK, HD), bf16),
            pltpu.VMEM((TOK, HD), bf16),
            pltpu.VMEM((Z, HALF, TOK), bf16),
            pltpu.VMEM((NF, HALF + 16, HD), f32),
            pltpu.VMEM((Z, HALF, HD), bf16),
            pltpu.VMEM((NF, HALF, HD), bf16),
            pltpu.VMEM((2, HALF, HD), bf16),
            pltpu.VMEM((2, HALF, HD), bf16),
            pltpu.VMEM((4, HALF, HD), bf16),
            pltpu.VMEM((3, NF, FAR, HD), bf16),
            pltpu.VMEM((3, NF, FAR, HD), bf16),
            pltpu.VMEM((4, NF, FAR, HD), bf16),
            pltpu.VMEM((HALF + 8, HD), f32),
            pltpu.VMEM((8, OWN, HD), bf16),
            pltpu.VMEM((NF, FAR + 8, HD), f32),
            pltpu.VMEM((NF, 2, OWN, HD), bf16),
            pltpu.VMEM((Y, OWN, HD), bf16),
            pltpu.VMEM((NF, OWN, HD), bf16),
            pltpu.VMEM((TOK, SHARE), bf16),
            pltpu.VMEM((8, 128), f32),
            pltpu.VMEM((15, 8, 128), f32),
            pltpu.VMEM((8, 128), f32),
            pltpu.VMEM((11, 8, 128), f32),
            dma((8,)), dma((4,)), dma((4,)),
            dma((3,)), dma((3,)), dma((3,)), dma((3,)), dma((3,)), dma((3,)),
            dma((Z + 1,)), dma((Z + 1,)), dma((6,)), dma((6,)), dma((14,)), dma((14,)),
            dma((16,)), dma((8,)), dma((10,)), dma((5,)), dma((15,)), dma((15,)),
            dma((11,)), dma((11,)),
        ],
        compiler_params=pltpu.CompilerParams(
            collective_id=0, has_side_effects=True, vmem_limit_bytes=24 << 20
        ),
    )(hidden, w_key, grad_key, gain, counts)


def per_device(hidden, gain, w_key, grad_key, counts):
    in_hbm = lambda v: pltpu.with_memory_space_constraint(v, pltpu.HBM)
    gain = gain.reshape(D // 128, 128)
    return fused(*(in_hbm(v) for v in (hidden, w_key, grad_key, gain)), counts)


def solution(mesh):
    split = Mesh(
        mesh.devices.reshape(Z, Y, 2, mesh.shape["tensor"]), ("dp_0", "dp_1", "dp_2", "tensor")
    )
    return jax.shard_map(
        per_device,
        mesh=split,
        in_specs=(P(DP, None), P(), P(None, "tensor"), P(DP, "tensor"), P(DP)),
        out_specs=(P(DP, "tensor"), P(DP, "tensor")),
        check_vma=False,
    )
```

time: 355 us -> 43.4 us (0.12)
  waiting for transfers between devices: 249 us -> 0 us
  blocking collectives: 56.5 us -> 0 us
  Pallas kernels: 0 us -> 40.5 us
  local copies, waits for them, and re-layouts: 16.7 us -> 1.4 us
  between operations: 15.6 us -> 1.29 us
  other arithmetic: 7.86 us -> 0 us
  starting transfers between devices: 4.86 us -> 0 us
    reduce_scatter x1 -> x0, waiting for transfers between devices: 249 us -> none  [own_tiles(): own = lax.psum_scatter(lines, axis, scatter_dimension=0, tiled=True)]
    psum x3 -> x0, blocking collectives: 56.5 us -> none  [one_axis_at_a_time(): return functools.reduce(lax.psum, axes, x)]
    pallas_call x0 -> x1, Pallas kernels: none -> 40.5 us  [fused(): pl.pallas_call(kernel, out_shape=(jax.ShapeDtypeStruct((ROWS, HD), f32),...]
    reshape x2 -> x0, local copies, waits for them, and re-layouts: 6.71 us -> none  [the longest x1 5.19 us: own_tiles(): jnp.pad(lines, ((0, 0), (0, span * 128 - lines.shape[1]))).reshape(-1, 128)]
    another operation x1 -> x0, local copies, waits for them, and re-layouts: 5.02 us -> none  [own_tiles(): lines = tiles.reshape(devices, -1)]
    pad x1 -> x0, local copies, waits for them, and re-layouts: 4.9 us -> none  [own_tiles(): jnp.pad(lines, ((0, 0), (0, span * 128 - lines.shape[1]))).reshape(-1, 128)]
    all_to_all x1 -> x0, starting transfers between devices: 4.83 us -> none  [sent_and_summed(): tiles = lax.all_to_all(cut_along(x, dim, devices), axis, 0, 0, tiled=True)]
    reduce_sum x2 -> x0, other arithmetic: 4.3 us -> none  [the longest x1 2.18 us: per_device(): jnp.mean(wide_hidden * wide_hidden, axis=1, keepdims=True) + EPSILON]
  transfers between devices with their start and end apart: 2 -> 0, of which waited for: 1 -> 0; matrix products, arithmetic and copies ran while one was open for 1% -> 0% of each run, Pallas kernels for 0% -> 0%
where the time goes in v3:
time: 43.4 us; the launch traced here: 43.2 us
  Pallas kernels  40.5 us (93%)
  local copies, waits for them, and re-layouts  1.4 us (3%)
  between operations  1.29 us (3%)
    pallas_call x1, Pallas kernels, fused(): pl.pallas_call(kernel, out_shape=(jax.ShapeDtypeStruct((ROWS, HD), f32),...  40.5 us
    unnamed x2, local copies, waits for them, and re-layouts  1.4 us

profile of v3, /device:TPU:1, one launch (start us, length us, event | category | flops | bytes accessed | tf_op | source)
XLA Modules:
  0.0 43.2 jit_solution(13872144063913673989)
XLA Ops:
  1.3 40.5 %shard_map.68 = (f32[43,128]{1,0:T(8,128)S(1)}, bf16[128,2048]{1,0:T(8,128)(2,1)S(1)}) custom-call(bf16[128,8192]{1,0:T(8,128)(2,1)} %hid_hbm.1, bf16[8192,128]{1,0:T(8,128)(2,1)} %w_hbm.1, bf16[128,128]{1,0:T(8,128)(2,1)} %gk_hbm.1, f32[64,128]{1,0:T(8,128)} %bitcast.1, s32[1]{0:T(128)S(6)} %copy.9.cnt_hbm), custom_call_target="tpu_custom_call" | custom-call | tf_op jit(solution)/shard_map/pallas_call | solution.py:408
  41.8 0.6 %copy.10 = f32[43,128]{1,0:T(8,128)} copy(f32[43,128]{1,0:T(8,128)S(1)} %get-tuple-element.4) | data formatting | bytes 44032
  42.4 0.8 %copy.11 = bf16[128,2048]{1,0:T(8,128)(2,1)} copy(bf16[128,2048]{1,0:T(8,128)(2,1)S(1)} %get-tuple-element.5) | data formatting | bytes 1048576

commit v4 on v3

--- a/solution.py
+++ b/solution.py
@@ -19,8 +19,9 @@
 OWN = 48
 FARS = (6, 5, 7, 4, 8)
 PARTS = ((0, 2, 1), (2, 5, -1))
-GROUPS = (FARS[:2], FARS[2:], (3, 9), (1, 11, 2, 10, 0))
+GROUPS = (FARS[:2], (3, 9), FARS[2:], (1, 11, 2, 10, 0))
 NF = len(FARS)
+PIECES = ((0, 12), (12, 24), (24, 36), (36, 48), (48, 56), (56, 60), (60, 64))
 SHARE = D // X
 
 
@@ -55,10 +56,9 @@
             device_id_type=MESH,
         )
 
-    PIECES = 8
     loads = []
-    for i in range(PIECES):
-        cols = pl.ds(i * (D // PIECES), D // PIECES)
+    for i, (first, last) in enumerate(PIECES):
+        cols = pl.ds(first * 128, (last - first) * 128)
         load = pltpu.make_async_copy(hid_hbm.at[:, cols], hid.at[:, cols], hid_sem.at[i])
         load.start()
         loads.append(load)
@@ -98,17 +98,17 @@
         shifted[s, HALF + 8 :, :] = jnp.zeros((8, 128), f32)
 
     squares = jnp.zeros((TOK, 128), f32)
-    for i in range(PIECES):
+    for i, (first, last) in enumerate(PIECES):
         loads[i].wait()
 
-        def add_squares(t, total, i=i):
-            lanes = pl.ds(pl.multiple_of(i * (D // PIECES) + t * 128, 128), 128)
+        def add_squares(t, total):
+            lanes = pl.ds(pl.multiple_of(t * 128, 128), 128)
             block = hid[:, lanes]
             turned[lanes, :] = block.T
             v = block.astype(f32)
             return total + v * v
 
-        squares = lax.fori_loop(0, D // PIECES // 128, add_squares, squares, unroll=4)
+        squares = lax.fori_loop(first, last, add_squares, squares, unroll=4)
     inv_rms = lax.rsqrt(jnp.sum(squares, axis=1, keepdims=True) * (1.0 / D) + EPSILON)
     live = lax.broadcasted_iota(jnp.int32, (TOK, HD), 0) < count
     gk_load.wait()
@@ -216,15 +216,16 @@
     finish(GROUPS[0], both)
     first_far(0)
     finish(GROUPS[1], both)
-    first_far(1)
-    finish(GROUPS[2], both)
     send_near(0, summed.at[3], near_mid.at[0], 1)
     send_near(1, summed.at[9], near_mid.at[1], 11)
+    finish(GROUPS[2], both)
+    first_far(1)
     finish(GROUPS[3], both)
     send_near(2, summed.at[1], near.at[0], 1)
     send_near(3, summed.at[11], near.at[1], 11)
 
-    for p, (first, last, way) in enumerate(PARTS):
+    def second_far(p):
+        first, last, way = PARTS[p]
         n = pl.ds(first, last - first)
         for m, r in enumerate((3 * way % Y, -2 * way % Y, way % Y)):
 
@@ -238,6 +239,8 @@
 
             send_far(7 * p + 4 + m, far_out.at[m, n], far.at[1 + m, n], r, r)
 
+    second_far(0)
+
     for n, (j, step) in enumerate(((2, 2), (10, 10))):
         near_sends[n].wait_recv()
 
@@ -248,6 +251,8 @@
 
         lax.fori_loop(0, HALF // 32, merge_near, 0, unroll=True)
         send_near(4 + n, near_out.at[n], near.at[2 + n], step)
+
+    second_far(1)
 
     for send in c1:
         send.wait_recv()
@@ -287,6 +292,20 @@
                     far_own[i, e] = far_f[i, pl.ds(inside + e * ROWS, OWN), :].astype(bf16)
                     f2[2 * i + e].start()
 
+    wf = []
+
+    def pass_on(n):
+        k, send = wx[n]
+        send.wait_recv()
+        forward = remote(
+            wbuf.at[k, upper, :], wbuf.at[k, upper, :], wf_s.at[k - 1], wf_r.at[k - 1], cc=1 - c
+        )
+        forward.start()
+        wf.append(forward)
+
+    pass_on(0)
+    pass_on(1)
+
     for i in (2, 3, 4, 5):
         near_sends[i].wait_recv()
 
@@ -319,14 +338,7 @@
     def _():
         near_in[0] = near_own[2 * quarter + c]
 
-    wf = []
-    for k, send in wx:
-        send.wait_recv()
-        forward = remote(
-            wbuf.at[k, upper, :], wbuf.at[k, upper, :], wf_s.at[k - 1], wf_r.at[k - 1], cc=1 - c
-        )
-        forward.start()
-        wf.append(forward)
+    pass_on(2)
 
     gain_load.wait()
     first = ROWS * ((z * Y + y) * 2 + c)
@@ -455,10 +467,33 @@
     )(hidden, w_key, grad_key, gain, counts)
 
 
+def put_out(kg, ng):
+    def body(kg_ref, ng_ref, kg_hbm, ng_hbm, sems):
+        copies = (
+            pltpu.make_async_copy(ng_ref, ng_hbm, sems.at[0]),
+            pltpu.make_async_copy(kg_ref, kg_hbm, sems.at[1]),
+        )
+        for copy in copies:
+            copy.start()
+        for copy in copies:
+            copy.wait()
+
+    anywhere = pl.BlockSpec(memory_space=pl.ANY)
+    hbm = pl.BlockSpec(memory_space=pltpu.HBM)
+    return pl.pallas_call(
+        body,
+        out_shape=tuple(jax.ShapeDtypeStruct(v.shape, v.dtype) for v in (kg, ng)),
+        in_specs=[anywhere] * 2,
+        out_specs=(hbm, hbm),
+        scratch_shapes=[pltpu.SemaphoreType.DMA((2,))],
+        compiler_params=pltpu.CompilerParams(vmem_limit_bytes=1 << 20),
+    )(kg, ng)
+
+
 def per_device(hidden, gain, w_key, grad_key, counts):
     in_hbm = lambda v: pltpu.with_memory_space_constraint(v, pltpu.HBM)
     gain = gain.reshape(D // 128, 128)
-    return fused(*(in_hbm(v) for v in (hidden, w_key, grad_key, gain)), counts)
+    return put_out(*fused(*(in_hbm(v) for v in (hidden, w_key, grad_key, gain)), counts))
 
 
 def solution(mesh):

time: 43.4 us -> 42.1 us (0.970)
  local copies, waits for them, and re-layouts: 1.4 us -> 0 us
    unnamed x2 -> x0, local copies, waits for them, and re-layouts: 1.4 us -> none
    pallas_call x0 -> x1, Pallas kernels: none -> 0.81 us  [put_out(): pl.pallas_call(body, out_shape=tuple((jax.ShapeDtypeStruct(v.shape, v.dty...]
    pallas_call x1, Pallas kernels: 40.5 us -> 39.9 us  [fused(): pl.pallas_call(kernel, out_shape=(jax.ShapeDtypeStruct((ROWS, HD), f32),...]
where the time goes in v4:
time: 42.1 us; the launch traced here: 42 us
  Pallas kernels  40.7 us (97%)
  between operations  1.29 us (3%)
    pallas_call x1, Pallas kernels, fused(): pl.pallas_call(kernel, out_shape=(jax.ShapeDtypeStruct((ROWS, HD), f32),...  39.9 us

profile of v4, /device:TPU:1, one launch (start us, length us, event | category | flops | bytes accessed | tf_op | source)
XLA Modules:
  0.0 42.0 jit_solution(6723159267610980279)
XLA Ops:
  1.3 39.9 %shard_map.68 = (f32[43,128]{1,0:T(8,128)S(1)}, bf16[128,2048]{1,0:T(8,128)(2,1)S(1)}) custom-call(bf16[128,8192]{1,0:T(8,128)(2,1)} %hid_hbm.1, bf16[8192,128]{1,0:T(8,128)(2,1)} %w_hbm.1, bf16[128,128]{1,0:T(8,128)(2,1)} %gk_hbm.1, f32[64,128]{1,0:T(8,128)} %bitcast.1, s32[1]{0:T(128)S(6)} %copy.7.cnt_hbm), custom_call_target="tpu_custom_call" | custom-call | tf_op jit(solution)/shard_map/pallas_call | solution.py:420
  41.2 0.8 %shard_map.69 = (f32[43,128]{1,0:T(8,128)}, bf16[128,2048]{1,0:T(8,128)(2,1)}) custom-call(f32[43,128]{1,0:T(8,128)S(1)} %get-tuple-element.4.kg_ref, bf16[128,2048]{1,0:T(8,128)(2,1)S(1)} %get-tuple-element.5.ng_ref), custom_call_target="tpu_custom_call" | custom-call | tf_op jit(solution)/shard_map/pallas_call | solution.py:483

commit v5 on v4

--- a/solution.py
+++ b/solution.py
@@ -117,7 +117,7 @@
     pl.semaphore_wait(barrier, greeted)
 
     near_sends, far_sends = {}, []
-    pairs, gx, wx, c1 = {}, [], [], []
+    pairs, gx, wx, c2 = {}, [], [], []
     upper = pl.ds(pl.multiple_of(c * (SHARE // 2), SHARE // 2), SHARE // 2)
 
     def window(target):
@@ -152,18 +152,11 @@
             send.start()
             gx.append(send)
 
-    def counts_along_y():
-        for d in range(Y):
-            for e in range(2):
-                if d + e == 0:
-                    continue
-                slot = 2 * d + e - 1
-                send = remote(
-                    cnt_own, cnt_in.at[slot], c1_s.at[slot], c1_r.at[slot],
-                    yy=at_y(d), cc=c if e == 0 else 1 - c,
-                )
-                send.start()
-                c1.append(send)
+    def counts_along_z():
+        for d in range(1, Z):
+            send = remote(cnt_own, cnt_in2.at[d - 1], c2_s.at[d - 1], c2_r.at[d - 1], zz=at_z(d))
+            send.start()
+            c2.append(send)
 
     def send_near(i, src, dst, step):
         near_sends[i] = remote(src, dst, near_s.at[i], near_r.at[i], zz=at_z(step))
@@ -197,7 +190,7 @@
         for j in group:
             share(j)
     weights_along_x()
-    counts_along_y()
+    counts_along_z()
     swap.wait_recv()
     both = jnp.concatenate([scaled[...], other[...]], axis=0)
     def first_far(p):
@@ -254,14 +247,21 @@
 
     second_far(1)
 
-    for send in c1:
+    for send in c2:
         send.wait_recv()
-    cnt_mid[...] = cnt_own[...] + jnp.sum(cnt_in[...], axis=0)
-    c2 = []
-    for d in range(1, Z):
-        send = remote(cnt_mid, cnt_in2.at[d - 1], c2_s.at[d - 1], c2_r.at[d - 1], zz=at_z(d))
-        send.start()
-        c2.append(send)
+    cnt_mid[...] = cnt_own[...] + jnp.sum(cnt_in2[...], axis=0)
+    c1 = []
+    for d in range(Y):
+        for e in range(2):
+            if d + e == 0:
+                continue
+            slot = 2 * d + e - 1
+            send = remote(
+                cnt_mid, cnt_in.at[slot], c1_s.at[slot], c1_r.at[slot],
+                yy=at_y(d), cc=c if e == 0 else 1 - c,
+            )
+            send.start()
+            c1.append(send)
 
     f2 = []
     for i, j in enumerate(FARS):
@@ -357,9 +357,9 @@
         send.wait_recv()
     for k in range(X):
         heads[k] = jnp.where(live, heads[k].astype(f32), 0.0).astype(bf16)
-    for send in c2:
+    for send in c1:
         send.wait_recv()
-    weighting = (1.0 * TOK * Z * Y * 2) / (cnt_mid[...] + jnp.sum(cnt_in2[...], axis=0))
+    weighting = (1.0 * TOK * Z * Y * 2) / (cnt_mid[...] + jnp.sum(cnt_in[...], axis=0))
     weight = weighting[0:1, 0:1]
     TILE = 512
     outs = []

time: 42.1 us -> 43 us (1.021)
  Pallas kernels: 40.7 us -> 41.5 us
    pallas_call x1, Pallas kernels: 39.9 us -> 40.7 us  [fused(): pl.pallas_call(kernel, out_shape=(jax.ShapeDtypeStruct((ROWS, HD), f32),...]
where the time goes in v5:
time: 43 us; the launch traced here: 42.8 us
  Pallas kernels  41.5 us (97%)
  between operations  1.29 us (3%)
    pallas_call x1, Pallas kernels, fused(): pl.pallas_call(kernel, out_shape=(jax.ShapeDtypeStruct((ROWS, HD), f32),...  40.7 us

profile of v5, /device:TPU:1, one launch (start us, length us, event | category | flops | bytes accessed | tf_op | source)
XLA Modules:
  0.0 42.8 jit_solution(18011848103078488170)
XLA Ops:
  1.3 40.7 %shard_map.68 = (f32[43,128]{1,0:T(8,128)S(1)}, bf16[128,2048]{1,0:T(8,128)(2,1)S(1)}) custom-call(bf16[128,8192]{1,0:T(8,128)(2,1)} %hid_hbm.1, bf16[8192,128]{1,0:T(8,128)(2,1)} %w_hbm.1, bf16[128,128]{1,0:T(8,128)(2,1)} %gk_hbm.1, f32[64,128]{1,0:T(8,128)} %bitcast.1, s32[1]{0:T(128)S(6)} %copy.7.cnt_hbm), custom_call_target="tpu_custom_call" | custom-call | tf_op jit(solution)/shard_map/pallas_call | solution.py:420
  42.0 0.8 %shard_map.69 = (f32[43,128]{1,0:T(8,128)}, bf16[128,2048]{1,0:T(8,128)(2,1)}) custom-call(f32[43,128]{1,0:T(8,128)S(1)} %get-tuple-element.4.kg_ref, bf16[128,2048]{1,0:T(8,128)(2,1)S(1)} %get-tuple-element.5.ng_ref), custom_call_target="tpu_custom_call" | custom-call | tf_op jit(solution)/shard_map/pallas_call | solution.py:483
